TPU v7x, 32 devices: a whole 2x2x4 slice. The times are simulated.
32 devices in a mesh: row: 4 (over y, x), col: 8 (over z, core).
Axes of the slice: x: 2, y: 2, z: 4, core: 2. Of those that a mesh axis runs over, the one named last changes fastest.
Arguments:
- trailing: float32 [3072, 3072], P('row', 'col'), may hold values from -6 to 6, as said below
- v_panels: bfloat16 [3, 3072, 256], P(None, ('row', 'col')), may hold values from -6 to 6
Outputs:
- updated: float32 [3072, 3072], P('row', 'col')
- w_panels: float32 [3, 3072, 256], P(None, ('row', 'col'))
Inputs may be any that keep to these rules, and one draw needn't show every extreme that they name: trailing is symmetric: entry (i, j) equals entry (j, i).
All inputs are finite; a program needn't handle non-finite values.
Results may differ from a plain program's by a relative error of at most 0.0003.
Values may be sent and summed in bfloat16 or wider, within the bound.
A program may use at most 64 MiB of HBM per device.

v0:
```python
import math

import jax
import jax.numpy as jnp
from jax import lax
from jax.sharding import PartitionSpec as P


def broadcast(value, axis, root):
    mine = lax.axis_index(axis) == root
    return lax.psum(jnp.where(mine, value, jnp.zeros_like(value)), axis)


def on_device(trailing, v_panels):
    rows_tile = trailing.shape[0]
    cols_tile = trailing.shape[1]
    count_row = lax.axis_size("row")
    full_order = rows_tile * count_row
    scaling = 1.0 / math.sqrt(full_order)
    group_ratio = rows_tile // cols_tile
    col_index = lax.axis_index("col")
    root_row = col_index // group_ratio
    offset = col_index % group_ratio * cols_tile
    ticks_all = v_panels.shape[0]
    highest = lax.Precision.HIGHEST
    v_rows_all = lax.all_gather(v_panels, "col", axis=1, tiled=True)
    v_mirror_all = broadcast(v_rows_all, "row", root_row)
    v_cols_all = lax.dynamic_slice_in_dim(v_mirror_all, offset, cols_tile, 1)
    current = trailing
    w_list = []
    for tick in range(ticks_all):
        v_rows = v_rows_all[tick]
        v_cols = v_cols_all[tick]
        v_rows_f = v_rows.astype(jnp.float32)
        v_cols_f = v_cols.astype(jnp.float32)
        block = current
        summed = lax.psum_scatter(
            jnp.dot(block, v_cols_f, precision=highest, preferred_element_type=jnp.float32),
            "col",
            scatter_dimension=0,
            tiled=True,
        )
        w_piece = summed * scaling
        w_rows = lax.all_gather(w_piece, "col", axis=0, tiled=True)
        w_mirror = broadcast(w_rows, "row", root_row)
        w_cols = lax.dynamic_slice_in_dim(w_mirror, offset, cols_tile, 0)
        rows_side = jnp.concatenate([v_rows_f, w_rows], axis=1)
        cols_side = jnp.concatenate([w_cols, v_cols_f], axis=1)
        update = lax.dot_general(
            rows_side,
            cols_side,
            (((1,), (1,)), ((), ())),
            precision=highest,
            preferred_element_type=jnp.float32,
        )
        current = current - update * (0.5 * scaling)
        w_list.append(w_piece)
    return (current, jnp.stack(w_list, axis=0))


def solution(mesh):
    in_specs = (P("row", "col"), P(None, ("row", "col"), None))
    out_specs = (P("row", "col"), P(None, ("row", "col"), None))
    return jax.shard_map(
        on_device, mesh=mesh, in_specs=in_specs, out_specs=out_specs, check_vma=False
    )
```

profile of v0, /device:TPU:25, one launch (start us, length us, event | category | flops | bytes accessed | tf_op | source)
XLA Modules:
  0.0 413.9 jit_solution(6455830931447291190)
XLA Ops:
  8.0 24.6 %all-gather.2.cloned.1.call-done = bf16[3,768,256]{2,1,0:T(8,128)(2,1)} async-done(((bf16[3,96,256]{2,1,0:T(8,128)(2,1)}), bf16[3,768,256]{2,1,0:T(8,128)(2,1)}) %all-gather.2.cloned.1.call-update) | async-done | bytes 1179664 | tf_op jit(solution)/shard_map/all_gather | solution.py:26
  32.6 1.1 broadcast_select_fusion
  33.8 57.2 %all-reduce.5.cloned.1.call-done = bf16[3,768,256]{2,1,0:T(8,128)(2,1)} async-done(((bf16[3,768,256]{2,1,0:T(8,128)(2,1)}), bf16[3,768,256]{2,1,0:T(8,128)(2,1)}) %all-reduce.5.cloned.1.call-update) | async-done | bytes 1179664 | tf_op jit(solution)/shard_map/psum | solution.py:11
  90.9 1.8 convolution_bitcast_fusion
  92.8 1.1 copy.16
  94.0 29.6 %reduce-scatter.10.cloned.1.call-done = f32[96,256]{1,0:T(8,128)} async-done(((f32[768,256]{1,0:T(8,128)}), f32[96,256]{1,0:T(8,128)}) %reduce-scatter.10.cloned.1.call-update) | async-done | bytes 98320
  125.3 16.2 %all_gather.13 = f32[768,256]{1,0:T(8,128)S(1)} all-gather(f32[96,256]{1,0:T(8,128)S(1)} %copy.8), channel_id=1, replica_groups=mesh['row'=4,'col'=8] {'col'}, dimensions={0}, use_global_device_ids=true | all-gather | bytes 884736 | tf_op jit(solution)/shard_map/all_gather | solution.py:44
  143.0 1.4 fusion.39
  146.0 45.8 %all-reduce.7.cloned.1.call-done = f32[768,256]{1,0:T(8,128)} async-done(((f32[768,256]{1,0:T(8,128)}), f32[768,256]{1,0:T(8,128)}) %all-reduce.7.cloned.1.call-update) | async-done | bytes 786448 | tf_op jit(solution)/shard_map/psum | solution.py:11
  191.8 1.1 constant_dynamic-slice_fusion.2
  193.0 3.6 fusion.27
  196.6 2.6 fusion.44
  199.3 29.5 %reduce-scatter.12.cloned.1.call-done = f32[96,256]{1,0:T(8,128)} async-done(((f32[768,256]{1,0:T(8,128)}), f32[96,256]{1,0:T(8,128)}) %reduce-scatter.12.cloned.1.call-update) | async-done | bytes 98320
  230.6 16.2 %all_gather.14 = f32[768,256]{1,0:T(8,128)S(1)} all-gather(f32[96,256]{1,0:T(8,128)S(1)} %copy.10), channel_id=1, replica_groups=mesh['row'=4,'col'=8] {'col'}, dimensions={0}, use_global_device_ids=true | all-gather | bytes 884736 | tf_op jit(solution)/shard_map/all_gather | solution.py:44
  247.7 49.2 %all-reduce.9.cloned.1.call-done = f32[768,256]{1,0:T(8,128)} async-done(((f32[768,256]{1,0:T(8,128)}), f32[768,256]{1,0:T(8,128)}) %all-reduce.9.cloned.1.call-update) | async-done | bytes 786448 | tf_op jit(solution)/shard_map/psum | solution.py:11
  297.0 1.0 constant_dynamic-slice_fusion.1
  298.0 3.9 fusion.21
  301.8 2.6 fusion.46
  304.5 29.5 %reduce-scatter.14.cloned.1.call-done = f32[96,256]{1,0:T(8,128)} async-done(((f32[768,256]{1,0:T(8,128)}), f32[96,256]{1,0:T(8,128)}) %reduce-scatter.14.cloned.1.call-update) | async-done | bytes 98320
  335.8 16.4 %all_gather.15 = f32[768,256]{1,0:T(8,128)S(1)} all-gather(f32[96,256]{1,0:T(8,128)S(1)} %copy.12), channel_id=1, replica_groups=mesh['row'=4,'col'=8] {'col'}, dimensions={0}, use_global_device_ids=true | all-gather | bytes 884736 | tf_op jit(solution)/shard_map/all_gather | solution.py:44
  353.1 1.1 pad_maximum_fusion
  355.1 47.2 %all-reduce.11.cloned.1.call-done = f32[768,256]{1,0:T(8,128)} async-done(((f32[768,256]{1,0:T(8,128)}), f32[768,256]{1,0:T(8,128)}) %all-reduce.11.cloned.1.call-update) | async-done | bytes 786448 | tf_op jit(solution)/shard_map/psum | solution.py:11
  402.4 1.0 constant_dynamic-slice_fusion
  403.4 3.6 fusion.15
  (40 shorter events, 12.3 us)
Async XLA Ops:
  7.2 25.4 %all-gather.2.cloned.1.call-start = ((), (), s32[]{:S(2)}) async-start(), calls=%async_computation.3 | async-start | bytes 1327104 | tf_op jit(solution)/shard_map/all_gather | solution.py:26
  7.9 83.0 %all-reduce.5.cloned.1.call-start = ((), (), s32[]{:S(2)}) async-start(), calls=%async_computation.4 | async-start | bytes 2359296 | tf_op jit(solution)/shard_map/psum | solution.py:11
  33.7 57.2 %copy-start.1 = (f32[768,384]{1,0:T(8,128)S(1)}, f32[768,384]{1,0:T(8,128)}, u32[]{:S(2)}) copy-start(f32[768,384]{1,0:T(8,128)} %param.2) | copy-start | bytes 3538948
  33.7 89.9 %reduce-scatter.10.cloned.1.call-start = ((), (), s32[]{:S(2)}) async-start(), calls=%async_computation.8 | async-start | bytes 884736
  93.9 97.8 %all-reduce.7.cloned.1.call-start = ((), (), s32[]{:S(2)}) async-start(), calls=%async_computation.5 | async-start | bytes 1572864 | tf_op jit(solution)/shard_map/psum | solution.py:11
  141.5 1.6 copy-start
  142.5 86.3 %reduce-scatter.12.cloned.1.call-start = ((), (), s32[]{:S(2)}) async-start(), calls=%async_computation.9 | async-start | bytes 884736
  143.0 2.0 copy-start.4
  191.8 1.3 copy-start.3
  199.2 97.7 %all-reduce.9.cloned.1.call-start = ((), (), s32[]{:S(2)}) async-start(), calls=%async_computation.6 | async-start | bytes 1572864 | tf_op jit(solution)/shard_map/psum | solution.py:11
  247.7 86.3 %reduce-scatter.14.cloned.1.call-start = ((), (), s32[]{:S(2)}) async-start(), calls=%async_computation.10 | async-start | bytes 884736
  304.5 97.9 %all-reduce.11.cloned.1.call-start = ((), (), s32[]{:S(2)}) async-start(), calls=%async_computation.7 | async-start | bytes 1572864 | tf_op jit(solution)/shard_map/psum | solution.py:11
  353.1 50.3 %copy-start.2 = (f32[768,256]{1,0:T(8,128)S(1)}, f32[768,256]{1,0:T(8,128)}, u32[]{:S(2)}) copy-start(f32[768,256]{1,0:T(8,128)} %get-tuple-element.9) | copy-start | bytes 2359300
Sparse Core Ops, SparseCore 0:
  9.6 22.9 all-gather.1
  36.3 54.6 all-reduce.4
  94.1 29.4 reduce-scatter.9
  142.6 49.1 all-reduce.6
  199.4 29.3 reduce-scatter.11
  247.8 49.0 all-reduce.8
  304.6 29.3 reduce-scatter.13
  353.2 49.0 all-reduce.10
where the time goes:
time: 416 us; the launch traced here: 414 us
  waiting for transfers between devices  313 us (75%)
  blocking collectives  48.7 us (12%)
  matrix products  18.1 us (4%)
  between operations  14.3 us (3%)
  other arithmetic  9.55 us (2%)
  local copies, waits for them, and re-layouts  9.55 us (2%)
    psum x4, waiting for transfers between devices, broadcast(): return lax.psum(jnp.where(mine, value, jnp.zeros_like(value)), axis)  199 us
    unnamed x11, waiting for transfers between devices  89.4 us
    all_gather x3, blocking collectives, on_device(): w_rows = lax.all_gather(w_piece, 'col', axis=0, tiled=True)  48.7 us
    all_gather x1, waiting for transfers between devices, on_device(): v_rows_all = lax.all_gather(v_panels, 'col', axis=1, tiled=True)  24.6 us
    dot_general x3, matrix products, on_device(): lax.dot_general(rows_side, cols_side, (((1,), (1,)), ((), ())), precision...  11.1 us
  transfers between devices with their start and end apart: 8, of which 8 were waited for; matrix products, arithmetic and copies ran while one was open for 1% of the time, Pallas kernels for 0%

commit v1 on v0

v1 whole, which is shorter than its diff:
```python
import functools
import math

import jax
import jax.numpy as jnp
from jax import lax
from jax.experimental import pallas as pl
from jax.experimental.pallas import tpu as pltpu
from jax.sharding import PartitionSpec as P

MESH = pl.DeviceIdType.MESH
NT = (((1,), (1,)), ((), ()))
NN = (((1,), (0,)), ((), ()))


def dot(a, b, dims):
    return lax.dot_general(a, b, dims, preferred_element_type=jnp.float32)


def kernel(
    nrow, ncol, ratio, scaling,
    a_ref, v_ref, out_ref, w_ref,
    b_ref, vr, vt, part, got, wc, wr,
    v_send, v_recv, vt_send, vt_recv, vx_send, vx_recv,
    rs_send, rs_recv, wc_send, wc_recv, wr_send, wr_recv, local_sem,
):
    ticks, piece, depth = v_ref.shape
    rows_tile, cols_tile = a_ref.shape
    links = ncol // ratio
    r = lax.axis_index("row")
    c = lax.axis_index("col")
    q = c // ratio
    j = c % ratio
    half = 0.5 * scaling

    def rows(at):
        return pl.ds(pl.multiple_of(at * piece, piece), piece)

    def remote(src, dst, send, recv, row, col):
        return pltpu.make_async_remote_copy(
            src_ref=src, dst_ref=dst, send_sem=send, recv_sem=recv,
            device_id=(row, col), device_id_type=MESH,
        )

    from_row, from_col = c // ratio, j * nrow + r
    to_row, to_col = c % nrow, r * ratio + c // nrow
    stays = jnp.logical_and(to_row == r, to_col == c)

    barrier = pltpu.get_barrier_semaphore()
    for i in range(1, nrow):
        pl.semaphore_signal(barrier, inc=1, device_id=((r + i) % nrow, c), device_id_type=MESH)
    for i in range(1, ncol):
        pl.semaphore_signal(barrier, inc=1, device_id=(r, (c + i) % ncol), device_id_type=MESH)

    @pl.when(jnp.logical_not(stays))
    def _():
        pl.semaphore_signal(barrier, inc=1, device_id=(from_row, from_col), device_id_type=MESH)
        pl.semaphore_signal(barrier, inc=1, device_id=(to_row, to_col), device_id_type=MESH)

    pl.semaphore_wait(barrier, nrow + ncol - 2 + jnp.where(stays, 0, 2))

    def v_out(t, i):
        return remote(
            v_ref.at[t], vr.at[t, rows(c)], v_send.at[t, i], v_recv.at[t, c],
            r, ((q + i) % links) * ratio + j,
        )

    def v_side(t, i, k):
        src_col = ((q + i) % links) * ratio + j
        src = v_ref.at[t] if i == 0 else vr.at[t, rows(src_col)]
        return remote(
            src, vr.at[t, rows(src_col)], vx_send.at[t, i, k - 1], v_recv.at[t, src_col],
            r, q * ratio + (j + k) % ratio,
        )

    def v_own(t):
        return pltpu.make_async_copy(v_ref.at[t], vr.at[t, rows(c)], v_recv.at[t, c])

    def v_in(t, col):
        return pltpu.make_async_copy(v_ref.at[t], vr.at[t, rows(col)], v_recv.at[t, col])

    def v_start(t):
        for i in range(1, links):
            v_out(t, i).start()
        for k in range(1, ratio):
            v_side(t, 0, k).start()
        v_own(t).start()

    vt_move = remote(v_ref, vt.at[:, rows(to_row)], vt_send, vt_recv, to_row, to_col)
    vt_in = pltpu.make_async_copy(v_ref, vt.at[:, rows(r)], vt_recv)

    v_start(0)

    @pl.when(stays)
    def _():
        vt_in.start()

    @pl.when(jnp.logical_not(stays))
    def _():
        vt_move.start()

    for t in range(1, ticks):
        v_start(t)

    b_ref[...] = a_ref[...].T

    def v_relay(t):
        for i in range(1, links):
            v_in(t, ((q + i) % links) * ratio + j).wait()
            for k in range(1, ratio):
                v_side(t, i, k).start()

    def v_finish(t):
        v_in(t, c).wait()
        for i in range(links):
            for k in range(1, ratio):
                v_in(t, ((q + i) % links) * ratio + (j + k) % ratio).wait()

    def rs_out(t, i):
        peer = (r + i) % nrow
        return remote(
            part.at[t, rows(peer)], got.at[t, rows(r)], rs_send.at[t, i], rs_recv.at[t, r], peer, c
        )

    def rs_in(t, peer):
        return pltpu.make_async_copy(
            part.at[t, rows(peer)], got.at[t, rows(peer)], rs_recv.at[t, peer]
        )

    def wc_out(t, i):
        peer = (r + i) % nrow
        spot = wc.at[t, :, rows(r)]
        return remote(spot, spot, wc_send.at[t, i], wc_recv.at[t, r], peer, c)

    def wc_in(t, peer):
        spot = wc.at[t, :, rows(peer)]
        return pltpu.make_async_copy(spot, spot, wc_recv.at[t, peer])

    def vt_out(t, i):
        peer = (r + i) % nrow
        spot = vt.at[t, rows(r)]
        return remote(spot, spot, vx_send.at[t, links + i - 1, 0], vx_recv.at[t, r], peer, c)

    def vt_got(t, peer):
        spot = vt.at[t, rows(peer)]
        return pltpu.make_async_copy(spot, spot, vx_recv.at[t, peer])

    source = q == r
    up = jnp.logical_and(q >= r, q < links - 1)
    down = jnp.logical_and(q <= r, q > 0)

    def wr_spot(t, seat, peer):
        return wr.at[t, :, rows(seat * nrow + peer)]

    def wr_out(t, i, way, first):
        peer = (r + i) % nrow
        src = wc.at[t, :, rows(peer)] if first else wr_spot(t, j, peer)
        if way == 0:
            col = c + ratio
        elif way == 1:
            col = c - ratio
        else:
            col = q * ratio + (j + way - 1) % ratio
        return remote(
            src, wr_spot(t, j, peer), wr_send.at[t, i, way], wr_recv.at[t, j * nrow + peer], r, col
        )

    def wr_in(t, seat, peer):
        spot = wr_spot(t, seat, peer)
        return pltpu.make_async_copy(spot, spot, wr_recv.at[t, seat * nrow + peer])

    def wr_keep(t, i):
        peer = (r + i) % nrow
        return pltpu.make_async_copy(
            wc.at[t, :, rows(peer)], wr_spot(t, j, peer), local_sem.at[t, i]
        )

    def wr_ways(t, i, first, act):
        @pl.when(up)
        def _():
            act(wr_out(t, i, 0, first))

        @pl.when(down)
        def _():
            act(wr_out(t, i, 1, first))

        for k in range(1, ratio):
            act(wr_out(t, i, 1 + k, first))

    def start(copy):
        copy.start()

    def wait_send(copy):
        copy.wait_send()

    def update_rows(t):
        out_ref[...] = (out_ref if t else a_ref)[...] - half * (
            dot(vr[t], wc[t, 0], NT) + dot(vr[t], wc[t, 1], NT)
            + dot(wr[t, 0], vt[t], NT) + dot(wr[t, 1], vt[t], NT)
        )

    for t in range(ticks):
        if t == 0:
            v_relay(0)
            v_finish(0)
        high = b_ref[...].astype(jnp.bfloat16)
        low = (b_ref[...] - high.astype(jnp.float32)).astype(jnp.bfloat16)
        part[t] = dot(high, vr[t], NN) + dot(low, vr[t], NN)
        for i in range(1, nrow):
            rs_out(t, i).start()
        if t:
            update_rows(t - 1)
        total = part[t, rows(r)]
        for i in range(1, nrow):
            peer = (r + i) % nrow
            rs_in(t, peer).wait()
            total = total + got[t, rows(peer)]
        total = total * scaling
        head = total.astype(jnp.bfloat16)
        wc[t, 0, rows(r)] = head
        wc[t, 1, rows(r)] = (total - head.astype(jnp.float32)).astype(jnp.bfloat16)
        for i in range(1, nrow):
            wc_out(t, i).start()
        if t == 0:
            @pl.when(stays)
            def _():
                vt_in.wait()

            @pl.when(jnp.logical_not(stays))
            def _():
                vt_move.wait()

        for i in range(1, nrow):
            vt_out(t, i).start()

        @pl.when(source)
        def _():
            for i in range(nrow):
                if i:
                    wc_in(t, (r + i) % nrow).wait()
                wr_ways(t, i, True, start)
                wr_keep(t, i).start()

        @pl.when(jnp.logical_not(source))
        def _():
            for i in range(nrow):
                wr_in(t, j, (r + i) % nrow).wait()
                wr_ways(t, i, False, start)
            for i in range(1, nrow):
                wc_in(t, (r + i) % nrow).wait()

        if t < ticks - 1:
            v_relay(t + 1)
            b_ref[...] -= half * (dot(wc[t, 0], vr[t], NT) + dot(wc[t, 1], vr[t], NT))
            v_finish(t + 1)

        for i in range(1, nrow):
            vt_got(t, (r + i) % nrow).wait()

        @pl.when(source)
        def _():
            for i in range(nrow):
                wr_keep(t, i).wait()

        for k in range(1, ratio):
            for i in range(nrow):
                wr_in(t, (j + k) % ratio, (r + i) % nrow).wait()
        if t < ticks - 1:
            b_ref[...] -= half * (dot(vt[t], wr[t, 0], NT) + dot(vt[t], wr[t, 1], NT))
        mine = rows(c)
        w_ref[t] = wr[t, 0, mine].astype(jnp.float32) + wr[t, 1, mine].astype(jnp.float32)
    update_rows(ticks - 1)

    for t in range(ticks):
        for i in range(1, links):
            v_out(t, i).wait_send()
        for i in range(links):
            for k in range(1, ratio):
                v_side(t, i, k).wait_send()
        for i in range(1, nrow):
            rs_out(t, i).wait_send()
            wc_out(t, i).wait_send()
            vt_out(t, i).wait_send()

        @pl.when(source)
        def _():
            for i in range(nrow):
                wr_ways(t, i, True, wait_send)

        @pl.when(jnp.logical_not(source))
        def _():
            for i in range(nrow):
                wr_ways(t, i, False, wait_send)


def on_device(trailing, v_panels):
    nrow = lax.axis_size("row")
    ncol = lax.axis_size("col")
    rows_tile, cols_tile = trailing.shape
    ticks, piece, depth = v_panels.shape
    ratio = rows_tile // cols_tile
    links = ncol // ratio
    scaling = 1.0 / math.sqrt(rows_tile * nrow)
    dma = pltpu.SemaphoreType.DMA
    vmem = pl.BlockSpec(memory_space=pltpu.VMEM)
    return pl.pallas_call(
        functools.partial(kernel, nrow, ncol, ratio, scaling),
        out_shape=(
            jax.ShapeDtypeStruct(trailing.shape, jnp.float32),
            jax.ShapeDtypeStruct(v_panels.shape, jnp.float32),
        ),
        in_specs=[vmem, vmem],
        out_specs=(vmem, vmem),
        scratch_shapes=[
            pltpu.VMEM((cols_tile, rows_tile), jnp.float32),
            pltpu.VMEM((ticks, rows_tile, depth), jnp.bfloat16),
            pltpu.VMEM((ticks, cols_tile, depth), jnp.bfloat16),
            pltpu.VMEM((ticks, cols_tile, depth), jnp.float32),
            pltpu.VMEM((ticks, cols_tile, depth), jnp.float32),
            pltpu.VMEM((ticks, 2, cols_tile, depth), jnp.bfloat16),
            pltpu.VMEM((ticks, 2, rows_tile, depth), jnp.bfloat16),
            dma((ticks, links)),
            dma((ticks, ncol)),
            dma,
            dma,
            dma((ticks, links + nrow, ratio)),
            dma((ticks, nrow)),
            dma((ticks, nrow)),
            dma((ticks, nrow)),
            dma((ticks, nrow)),
            dma((ticks, nrow)),
            dma((ticks, nrow, ratio + 1)),
            dma((ticks, ncol)),
            dma((ticks, nrow)),
        ],
        compiler_params=pltpu.CompilerParams(collective_id=0, has_side_effects=True),
    )(trailing, v_panels)


def solution(mesh):
    in_specs = (P("row", "col"), P(None, ("row", "col"), None))
    out_specs = (P("row", "col"), P(None, ("row", "col"), None))
    return jax.shard_map(
        on_device, mesh=mesh, in_specs=in_specs, out_specs=out_specs, check_vma=False
    )
```

time: 416 us -> 113 us (0.27)
  waiting for transfers between devices: 313 us -> 0 us
  Pallas kernels: 0 us -> 109 us
  blocking collectives: 48.7 us -> 0 us
  matrix products: 18.1 us -> 0 us
  between operations: 14.3 us -> 0.65 us
  other arithmetic: 9.55 us -> 0 us
  local copies, waits for them, and re-layouts: 9.55 us -> 3.12 us
    psum x4 -> x0, waiting for transfers between devices: 199 us -> none  [broadcast(): return lax.psum(jnp.where(mine, value, jnp.zeros_like(value)), axis)]
    pallas_call x0 -> x1, Pallas kernels: none -> 109 us  [on_device(): pl.pallas_call(functools.partial(kernel, nrow, ncol, ratio, scaling), out...]
    unnamed x11 -> x0, waiting for transfers between devices: 89.4 us -> none
    all_gather x3 -> x0, blocking collectives: 48.7 us -> none  [on_device(): w_rows = lax.all_gather(w_piece, 'col', axis=0, tiled=True)]
    all_gather x1 -> x0, waiting for transfers between devices: 24.6 us -> none  [on_device(): v_rows_all = lax.all_gather(v_panels, 'col', axis=1, tiled=True)]
    dot_general x4 -> x0, matrix products: 12.9 us -> none  [the longest x3 11.1 us: on_device(): lax.dot_general(rows_side, cols_side, (((1,), (1,)), ((), ())), precision...]
    unnamed x2 -> x0, matrix products: 5.19 us -> none
  transfers between devices with their start and end apart: 8 -> 0, of which waited for: 8 -> 0; matrix products, arithmetic and copies ran while one was open for 1% -> 0% of each run, Pallas kernels for 0% -> 0%
where the time goes in v1:
time: 113 us
  Pallas kernels  109 us (96%)
  local copies, waits for them, and re-layouts  3.12 us (3%)
    pallas_call x1, Pallas kernels, on_device(): pl.pallas_call(functools.partial(kernel, nrow, ncol, ratio, scaling), out...  109 us
    unnamed x4, local copies, waits for them, and re-layouts  3.12 us

profile of v1, /device:TPU:25, one launch (start us, length us, event | category | flops | bytes accessed | tf_op | source)
XLA Modules:
  0.0 112.7 jit_solution(9002249546275120021)
XLA Ops:
  0.6 108.9 %shard_map.41 = (f32[768,384]{1,0:T(8,128)}, f32[3,96,256]{2,1,0:T(8,128)}) custom-call(f32[768,384]{1,0:T(8,128)} %a_ref.1, bf16[3,96,256]{2,1,0:T(8,128)(2,1)} %v_ref.1), custom_call_target="tpu_custom_call" | custom-call | tf_op jit(solution)/shard_map/pallas_call | solution.py:306
  109.6 0.0 copy-start
  109.6 2.4 %copy.6 = f32[768,384]{1,0:T(8,128)} copy(f32[768,384]{1,0:T(8,128)} %get-tuple-element.4) | data formatting | bytes 2359296
  112.0 0.0 copy-done
  112.0 0.7 copy.7
Async XLA Ops:
  109.6 2.4 %copy-start = (f32[3,96,256]{2,1,0:T(8,128)S(1)}, f32[3,96,256]{2,1,0:T(8,128)}, u32[]{:S(2)}) copy-start(f32[3,96,256]{2,1,0:T(8,128)} %get-tuple-element.5) | copy-start | bytes 884740

commit v2 on v1

--- a/solution.py
+++ b/solution.py
@@ -9,6 +9,7 @@
 from jax.sharding import PartitionSpec as P
 
 MESH = pl.DeviceIdType.MESH
+SPLITS = 3
 NT = (((1,), (1,)), ((), ()))
 NN = (((1,), (0,)), ((), ()))
 
@@ -33,8 +34,14 @@
     j = c % ratio
     half = 0.5 * scaling
 
+    splits = rs_recv.shape[1]
+    chunk = piece // splits
+
     def rows(at):
         return pl.ds(pl.multiple_of(at * piece, piece), piece)
+
+    def some(at, s):
+        return pl.ds(pl.multiple_of(at * piece + s * chunk, chunk), chunk)
 
     def remote(src, dst, send, recv, row, col):
         return pltpu.make_async_remote_copy(
@@ -116,25 +123,26 @@
             for k in range(1, ratio):
                 v_in(t, ((q + i) % links) * ratio + (j + k) % ratio).wait()
 
-    def rs_out(t, i):
+    def rs_out(t, s, i):
         peer = (r + i) % nrow
         return remote(
-            part.at[t, rows(peer)], got.at[t, rows(r)], rs_send.at[t, i], rs_recv.at[t, r], peer, c
-        )
-
-    def rs_in(t, peer):
+            part.at[t, some(peer, s)], got.at[t, some(r, s)],
+            rs_send.at[t, s, i], rs_recv.at[t, s, r], peer, c,
+        )
+
+    def rs_in(t, s, peer):
         return pltpu.make_async_copy(
-            part.at[t, rows(peer)], got.at[t, rows(peer)], rs_recv.at[t, peer]
-        )
-
-    def wc_out(t, i):
-        peer = (r + i) % nrow
-        spot = wc.at[t, :, rows(r)]
-        return remote(spot, spot, wc_send.at[t, i], wc_recv.at[t, r], peer, c)
-
-    def wc_in(t, peer):
-        spot = wc.at[t, :, rows(peer)]
-        return pltpu.make_async_copy(spot, spot, wc_recv.at[t, peer])
+            part.at[t, some(peer, s)], got.at[t, some(peer, s)], rs_recv.at[t, s, peer]
+        )
+
+    def wc_out(t, s, i):
+        peer = (r + i) % nrow
+        spot = wc.at[t, :, some(r, s)]
+        return remote(spot, spot, wc_send.at[t, s, i], wc_recv.at[t, s, r], peer, c)
+
+    def wc_in(t, s, peer):
+        spot = wc.at[t, :, some(peer, s)]
+        return pltpu.make_async_copy(spot, spot, wc_recv.at[t, s, peer])
 
     def vt_out(t, i):
         peer = (r + i) % nrow
@@ -149,12 +157,13 @@
     up = jnp.logical_and(q >= r, q < links - 1)
     down = jnp.logical_and(q <= r, q > 0)
 
-    def wr_spot(t, seat, peer):
-        return wr.at[t, :, rows(seat * nrow + peer)]
-
-    def wr_out(t, i, way, first):
-        peer = (r + i) % nrow
-        src = wc.at[t, :, rows(peer)] if first else wr_spot(t, j, peer)
+    def wr_spot(t, s, seat, peer):
+        return wr.at[t, :, some(seat * nrow + peer, s)]
+
+    def wr_out(t, s, i, way, first):
+        peer = (r + i) % nrow
+        spot = wr_spot(t, s, j, peer)
+        src = wc.at[t, :, some(peer, s)] if first else spot
         if way == 0:
             col = c + ratio
         elif way == 1:
@@ -162,30 +171,30 @@
         else:
             col = q * ratio + (j + way - 1) % ratio
         return remote(
-            src, wr_spot(t, j, peer), wr_send.at[t, i, way], wr_recv.at[t, j * nrow + peer], r, col
-        )
-
-    def wr_in(t, seat, peer):
-        spot = wr_spot(t, seat, peer)
-        return pltpu.make_async_copy(spot, spot, wr_recv.at[t, seat * nrow + peer])
-
-    def wr_keep(t, i):
+            src, spot, wr_send.at[t, s, i, way], wr_recv.at[t, s, j * nrow + peer], r, col
+        )
+
+    def wr_in(t, s, seat, peer):
+        spot = wr_spot(t, s, seat, peer)
+        return pltpu.make_async_copy(spot, spot, wr_recv.at[t, s, seat * nrow + peer])
+
+    def wr_keep(t, s, i):
         peer = (r + i) % nrow
         return pltpu.make_async_copy(
-            wc.at[t, :, rows(peer)], wr_spot(t, j, peer), local_sem.at[t, i]
-        )
-
-    def wr_ways(t, i, first, act):
+            wc.at[t, :, some(peer, s)], wr_spot(t, s, j, peer), local_sem.at[t, s, i]
+        )
+
+    def wr_ways(t, s, i, first, act):
         @pl.when(up)
         def _():
-            act(wr_out(t, i, 0, first))
+            act(wr_out(t, s, i, 0, first))
 
         @pl.when(down)
         def _():
-            act(wr_out(t, i, 1, first))
+            act(wr_out(t, s, i, 1, first))
 
         for k in range(1, ratio):
-            act(wr_out(t, i, 1 + k, first))
+            act(wr_out(t, s, i, 1 + k, first))
 
     def start(copy):
         copy.start()
@@ -193,34 +202,51 @@
     def wait_send(copy):
         copy.wait_send()
 
-    def update_rows(t):
+    def seat_rows(seat):
+        return pl.ds(pl.multiple_of(seat * cols_tile, cols_tile), cols_tile)
+
+    def update_v(t):
         out_ref[...] = (out_ref if t else a_ref)[...] - half * (
             dot(vr[t], wc[t, 0], NT) + dot(vr[t], wc[t, 1], NT)
-            + dot(wr[t, 0], vt[t], NT) + dot(wr[t, 1], vt[t], NT)
-        )
+        )
+
+    def update_w(t, seat):
+        at = seat_rows(seat)
+        out_ref[at] -= half * (dot(wr[t, 0, at], vt[t], NT) + dot(wr[t, 1, at], vt[t], NT))
+
+    def turn_w(t, seat):
+        at = seat_rows(seat)
+        b_ref[:, at] -= half * (dot(vt[t], wr[t, 0, at], NT) + dot(vt[t], wr[t, 1, at], NT))
 
     for t in range(ticks):
+        last = t == ticks - 1
         if t == 0:
             v_relay(0)
             v_finish(0)
         high = b_ref[...].astype(jnp.bfloat16)
         low = (b_ref[...] - high.astype(jnp.float32)).astype(jnp.bfloat16)
         part[t] = dot(high, vr[t], NN) + dot(low, vr[t], NN)
-        for i in range(1, nrow):
-            rs_out(t, i).start()
-        if t:
-            update_rows(t - 1)
-        total = part[t, rows(r)]
-        for i in range(1, nrow):
-            peer = (r + i) % nrow
-            rs_in(t, peer).wait()
-            total = total + got[t, rows(peer)]
-        total = total * scaling
-        head = total.astype(jnp.bfloat16)
-        wc[t, 0, rows(r)] = head
-        wc[t, 1, rows(r)] = (total - head.astype(jnp.float32)).astype(jnp.bfloat16)
-        for i in range(1, nrow):
-            wc_out(t, i).start()
+        for s in range(splits):
+            for i in range(1, nrow):
+                rs_out(t, s, i).start()
+        for s in range(splits):
+            total = part[t, some(r, s)]
+            for i in range(1, nrow):
+                peer = (r + i) % nrow
+                rs_in(t, s, peer).wait()
+                total = total + got[t, some(peer, s)]
+            total = total * scaling
+            head = total.astype(jnp.bfloat16)
+            wc[t, 0, some(r, s)] = head
+            wc[t, 1, some(r, s)] = (total - head.astype(jnp.float32)).astype(jnp.bfloat16)
+            for i in range(1, nrow):
+                wc_out(t, s, i).start()
+
+            @pl.when(source)
+            def _():
+                wr_ways(t, s, 0, True, start)
+                wr_keep(t, s, 0).start()
+
         if t == 0:
             @pl.when(stays)
             def _():
@@ -232,24 +258,35 @@
 
         for i in range(1, nrow):
             vt_out(t, i).start()
+        if t:
+            update_v(t - 1)
+            for seat in range(ratio):
+                update_w(t - 1, seat)
 
         @pl.when(source)
         def _():
-            for i in range(nrow):
-                if i:
-                    wc_in(t, (r + i) % nrow).wait()
-                wr_ways(t, i, True, start)
-                wr_keep(t, i).start()
+            for s in range(splits):
+                for i in range(1, nrow):
+                    wc_in(t, s, (r + i) % nrow).wait()
+                    wr_ways(t, s, i, True, start)
+                    wr_keep(t, s, i).start()
 
         @pl.when(jnp.logical_not(source))
         def _():
-            for i in range(nrow):
-                wr_in(t, j, (r + i) % nrow).wait()
-                wr_ways(t, i, False, start)
-            for i in range(1, nrow):
-                wc_in(t, (r + i) % nrow).wait()
-
-        if t < ticks - 1:
+            for s in range(splits):
+                wr_in(t, s, j, r).wait()
+                wr_ways(t, s, 0, False, start)
+            for s in range(splits):
+                for i in range(1, nrow):
+                    wr_in(t, s, j, (r + i) % nrow).wait()
+                    wr_ways(t, s, i, False, start)
+            for s in range(splits):
+                for i in range(1, nrow):
+                    wc_in(t, s, (r + i) % nrow).wait()
+
+        if last:
+            update_v(t)
+        else:
             v_relay(t + 1)
             b_ref[...] -= half * (dot(wc[t, 0], vr[t], NT) + dot(wc[t, 1], vr[t], NT))
             v_finish(t + 1)
@@ -259,17 +296,22 @@
 
         @pl.when(source)
         def _():
-            for i in range(nrow):
-                wr_keep(t, i).wait()
-
-        for k in range(1, ratio):
-            for i in range(nrow):
-                wr_in(t, (j + k) % ratio, (r + i) % nrow).wait()
-        if t < ticks - 1:
-            b_ref[...] -= half * (dot(vt[t], wr[t, 0], NT) + dot(vt[t], wr[t, 1], NT))
+            for s in range(splits):
+                for i in range(nrow):
+                    wr_keep(t, s, i).wait()
+
+        for k in range(ratio):
+            seat = (j + k) % ratio
+            if k:
+                for s in range(splits):
+                    for i in range(nrow):
+                        wr_in(t, s, seat, (r + i) % nrow).wait()
+            if last:
+                update_w(t, seat)
+            else:
+                turn_w(t, seat)
         mine = rows(c)
         w_ref[t] = wr[t, 0, mine].astype(jnp.float32) + wr[t, 1, mine].astype(jnp.float32)
-    update_rows(ticks - 1)
 
     for t in range(ticks):
         for i in range(1, links):
@@ -278,19 +320,22 @@
             for k in range(1, ratio):
                 v_side(t, i, k).wait_send()
         for i in range(1, nrow):
-            rs_out(t, i).wait_send()
-            wc_out(t, i).wait_send()
             vt_out(t, i).wait_send()
+            for s in range(splits):
+                rs_out(t, s, i).wait_send()
+                wc_out(t, s, i).wait_send()
 
         @pl.when(source)
         def _():
-            for i in range(nrow):
-                wr_ways(t, i, True, wait_send)
+            for s in range(splits):
+                for i in range(nrow):
+                    wr_ways(t, s, i, True, wait_send)
 
         @pl.when(jnp.logical_not(source))
         def _():
-            for i in range(nrow):
-                wr_ways(t, i, False, wait_send)
+            for s in range(splits):
+                for i in range(nrow):
+                    wr_ways(t, s, i, False, wait_send)
 
 
 def on_device(trailing, v_panels):
@@ -300,6 +345,7 @@
     ticks, piece, depth = v_panels.shape
     ratio = rows_tile // cols_tile
     links = ncol // ratio
+    splits = SPLITS if piece % (SPLITS * 16) == 0 else 1
     scaling = 1.0 / math.sqrt(rows_tile * nrow)
     dma = pltpu.SemaphoreType.DMA
     vmem = pl.BlockSpec(memory_space=pltpu.VMEM)
@@ -325,13 +371,13 @@
             dma,
             dma((ticks, links + nrow, ratio)),
             dma((ticks, nrow)),
-            dma((ticks, nrow)),
-            dma((ticks, nrow)),
-            dma((ticks, nrow)),
-            dma((ticks, nrow)),
-            dma((ticks, nrow, ratio + 1)),
-            dma((ticks, ncol)),
-            dma((ticks, nrow)),
+            dma((ticks, splits, nrow)),
+            dma((ticks, splits, nrow)),
+            dma((ticks, splits, nrow)),
+            dma((ticks, splits, nrow)),
+            dma((ticks, splits, nrow, ratio + 1)),
+            dma((ticks, splits, ncol)),
+            dma((ticks, splits, nrow)),
         ],
         compiler_params=pltpu.CompilerParams(collective_id=0, has_side_effects=True),
     )(trailing, v_panels)

time: 113 us -> 99.2 us (0.88)
  Pallas kernels: 109 us -> 94.5 us
    pallas_call x1, Pallas kernels: 109 us -> 94.5 us  [on_device(): pl.pallas_call(functools.partial(kernel, nrow, ncol, ratio, scaling), out...]
where the time goes in v2:
time: 99.2 us; the launch traced here: 98.3 us
  Pallas kernels  94.5 us (95%)
  local copies, waits for them, and re-layouts  3.12 us (3%)
    pallas_call x1, Pallas kernels, on_device(): pl.pallas_call(functools.partial(kernel, nrow, ncol, ratio, scaling), out...  94.5 us
    unnamed x4, local copies, waits for them, and re-layouts  3.12 us

profile of v2, /device:TPU:25, one launch (start us, length us, event | category | flops | bytes accessed | tf_op | source)
XLA Modules:
  0.0 98.3 jit_solution(13643091574932612609)
XLA Ops:
  0.6 94.5 %shard_map.41 = (f32[768,384]{1,0:T(8,128)}, f32[3,96,256]{2,1,0:T(8,128)}) custom-call(f32[768,384]{1,0:T(8,128)} %a_ref.1, bf16[3,96,256]{2,1,0:T(8,128)(2,1)} %v_ref.1), custom_call_target="tpu_custom_call" | custom-call | tf_op jit(solution)/shard_map/pallas_call | solution.py:352
  95.2 0.0 copy-start
  95.2 2.4 %copy.6 = f32[768,384]{1,0:T(8,128)} copy(f32[768,384]{1,0:T(8,128)} %get-tuple-element.4) | data formatting | bytes 2359296
  97.6 0.0 copy-done
  97.6 0.7 copy.7
Async XLA Ops:
  95.2 2.4 %copy-start = (f32[3,96,256]{2,1,0:T(8,128)S(1)}, f32[3,96,256]{2,1,0:T(8,128)}, u32[]{:S(2)}) copy-start(f32[3,96,256]{2,1,0:T(8,128)} %get-tuple-element.5) | copy-start | bytes 884740
